TPU v7x, 512 devices: a whole 4x4x16 slice. The times are simulated.
512 devices in a mesh: band: 16 (over x, y), region: 32 (over z, core).
Axes of the slice: x: 4, y: 4, z: 16, core: 2. Of those that a mesh axis runs over, the one named last changes fastest.
Arguments:
- state: bfloat16 [16, 32768], P(None, 'region'), may hold values from -4 to 4
- absorb_weight: bfloat16 [16, 16384], P(None, 'band'), may hold values from -1.5 to 1.5
- emit_weight: bfloat16 [16, 16384], P(None, 'band'), may hold values from -1.5 to 1.5
- path_len: float32 [8, 8192], P(None, 'region'), may hold values from 0.02 to 0.2
- crossing_slot: int32 [8, 8192], P(None, 'region'), may hold values from 0 to 4095, as said below
- request_rows: int32 [32, 32, 128], P('region'), may hold values from 0 to 1023
- cot_intensity: float32 [16384, 8192], P('band', 'region'), may hold values from -6 to 6
Outputs:
- grad_state: float32 [16, 32768], P(None, 'region')
Inputs may be any that keep to these rules, and one draw needn't show every extreme that they name: `crossing_slot`: within each ray block (the 256 rays of one index of region) the 2048 crossings take distinct slots; slot p * 128 + s names the cell listed at request_rows[block, p, s]. In every draw one region has all 128 of its slots taken by every ray block; the other listed slots are partly unused.
All inputs are finite; a program needn't handle non-finite values.
Results may differ from a plain program's by a relative error of at most 0.0051.
Values may be sent and summed in bfloat16 or wider, within the bound.
No kernel may reach another device: no remote copies, remote signals or barrier semaphores. Data moves between devices by JAX's collectives and lax.ppermute only.
A program may use at most 64 MiB of HBM per device.

v0:
```python
import jax
import jax.numpy as jnp
from jax import lax
from jax.sharding import PartitionSpec as P


def adjoint_block(absorb_x, emit_x, length, cot_block, w_abs, w_emit):
    depth_step = absorb_x.astype(jnp.float32) * length[None]
    passed = jnp.cumsum(depth_step, axis=1) - depth_step
    transmit = jnp.exp(-passed)
    emitted = emit_x.astype(jnp.float32) * length[None] * transmit
    behind = lax.cumsum(emitted, axis=1, reverse=True) - emitted
    grad_emit = (cot_block[:, None, :] * emitted).astype(jnp.bfloat16)
    grad_absorb = (-cot_block[:, None, :] * depth_step * behind).astype(jnp.bfloat16)
    bin_count = grad_emit.shape[0]
    grad_emit = grad_emit.reshape(bin_count, -1)
    grad_absorb = grad_absorb.reshape(bin_count, -1)
    return jnp.dot(w_abs, grad_absorb, preferred_element_type=jnp.float32) + jnp.dot(
        w_emit, grad_emit, preferred_element_type=jnp.float32
    )


def on_device(
    state, absorb_weight, emit_weight, path_len, crossing_slot, request_rows, cot_intensity
):
    bin_count = absorb_weight.shape[1]
    state_count = state.shape[0]
    cross_len = path_len.shape[0]
    ray_count = path_len.shape[1]
    wanted = lax.all_to_all(
        request_rows, "region", split_axis=1, concat_axis=0, tiled=True
    ).reshape(-1)
    slot_ids = crossing_slot.reshape(-1)
    picked = jnp.take(state, wanted, axis=1)
    arrived = lax.all_to_all(picked, "region", split_axis=1, concat_axis=1, tiled=True)
    state_x = jnp.take(arrived, slot_ids, axis=1)
    absorb_x = jnp.exp(
        jnp.dot(absorb_weight.T, state_x, preferred_element_type=jnp.float32)
    ).astype(jnp.bfloat16)
    emit_x = jnp.exp(jnp.dot(emit_weight.T, state_x, preferred_element_type=jnp.float32)).astype(
        jnp.bfloat16
    )
    bin_block = 256
    summed = jnp.zeros((state_count, cross_len * ray_count), jnp.float32)
    for first_bin in range(0, bin_count, bin_block):
        last_bin = first_bin + bin_block
        summed = summed + adjoint_block(
            absorb_x[first_bin:last_bin].reshape(bin_block, cross_len, ray_count),
            emit_x[first_bin:last_bin].reshape(bin_block, cross_len, ray_count),
            path_len,
            cot_intensity[first_bin:last_bin],
            absorb_weight[:, first_bin:last_bin],
            emit_weight[:, first_bin:last_bin],
        )
    sending = jnp.zeros((state_count, wanted.shape[0]), jnp.float32).at[:, slot_ids].set(summed)
    returned = lax.all_to_all(sending, "region", split_axis=1, concat_axis=1, tiled=True)
    partial_value = (
        jnp.zeros((state_count, state.shape[1]), jnp.float32).at[:, wanted].add(returned)
    )
    partial_value = lax.psum(partial_value, "band")
    return partial_value


def solution(mesh):
    return jax.shard_map(
        on_device,
        mesh=mesh,
        in_specs=(
            P(None, "region"),
            P(None, "band"),
            P(None, "band"),
            P(None, "region"),
            P(None, "region"),
            P("region", None, None),
            P("band", "region"),
        ),
        out_specs=P(None, "region"),
        check_vma=False,
    )
```

profile of v0, /device:TPU:32, one launch (start us, length us, event | category | flops | bytes accessed | tf_op | source)
XLA Modules:
  0.0 268.6 jit_solution(6498890352738340585)
XLA Ops:
  6.5 15.5 %all-to-all-start = ((s32[1,32,128]{2,0,1:T(1,128)}), s32[1,32,128]{2,0,1:T(1,128)S(1)}, u32[]{:S(2)}, u32[]{:S(2)}) async-start(s32[1,32,128]{2,0,1:T(1,128)} %bitcast.180), calls=%async_computation | async-start | bytes 32768 | tf_op jit(solution)/shard_map/all_to_all | solution.py:30
  22.0 0.7 copy.52
  23.3 0.9 copy.36
  24.3 8.9 %all-to-all-done = s32[1,32,128]{2,0,1:T(1,128)S(1)} async-done(((s32[1,32,128]{2,0,1:T(1,128)}), s32[1,32,128]{2,0,1:T(1,128)S(1)}, u32[]{:S(2)}, u32[]{:S(2)}) %all-to-all-start) | async-done | bytes 16416 | tf_op jit(solution)/shard_map/all_to_all | solution.py:30
  33.8 12.1 %gather_fusion = bf16[4096,16]{1,0:T(8,128)(2,1)S(1)} fusion(bf16[16,1024]{0,1:T(8,128)(2,1)S(1)} %copy.36, s32[4096]{0:T(1024)S(1)} %broadcast_clamp_fusion), kind=kCustom, calls=%fused_computation | custom fusion | bytes 278528 | tf_op jit(solution)/shard_map/jit(_take)/gather | solution.py:34
  47.0 5.0 %all-to-all-start.1 = ((bf16[16,32,128]{2,0,1:T(8,128)(2,1)}), bf16[16,32,128]{2,0,1:T(8,128)(2,1)S(1)}, u32[]{:S(2)}, u32[]{:S(2)}) async-start(bf16[16,32,128]{2,0,1:T(8,128)(2,1)} %broadcast_select_fusion.3), calls=%async_computation.1 | async-start | bytes 262144 | tf_op jit(solution)/shard_map/all_to_all | solution.py:35
  53.2 0.8 copy.43
  55.2 12.8 %all-to-all-done.1 = bf16[16,32,128]{2,0,1:T(8,128)(2,1)S(1)} async-done(((bf16[16,32,128]{2,0,1:T(8,128)(2,1)}), bf16[16,32,128]{2,0,1:T(8,128)(2,1)S(1)}, u32[]{:S(2)}, u32[]{:S(2)}) %all-to-all-start.1) | async-done | bytes 131104 | tf_op jit(solution)/shard_map/all_to_all | solution.py:35
  68.6 7.3 %gather_fusion.1 = bf16[2048,16]{1,0:T(8,128)(2,1)S(1)} fusion(bf16[16,4096]{0,1:T(8,128)(2,1)S(1)} %bitcast.166, s32[2048]{0:T(1024)} %broadcast_clamp_fusion.1), kind=kCustom, calls=%fused_computation.1 | custom fusion | bytes 139264 | tf_op jit(solution)/shard_map/jit(_take)/gather | solution.py:36
  75.9 2.4 fusion
  78.4 1.6 fusion.1
  80.0 0.7 slice_convert_fusion
  80.7 0.7 slice_convert_fusion.1
  82.1 0.9 fusion.35
  83.0 0.9 fusion.29
  84.0 2.5 fusion.5
  88.0 0.9 fusion.41
  89.0 0.9 fusion.47
  89.8 2.6 fusion.17
  95.2 6.2 %scatter_custom_fusion = f32[16,4096]{0,1:T(8,128)S(1)} fusion(s32[2048]{0:T(1024)} %bitcast.177, f32[2048,16]{1,0:T(8,128)S(1)} %copy.46, f32[]{:T(128)} %constant.41.clone.1), kind=kCustom, calls=%fused_computation.107 | custom fusion | bytes 262656 | tf_op jit(solution)/shard_map/scatter | solution.py:55
  102.0 25.2 %all_to_all.30 = f32[16,32,128]{2,0,1:T(8,128)S(1)} all-to-all(f32[16,32,128]{2,0,1:T(8,128)S(1)} %copy.47), channel_id=1, replica_groups=mesh['band'=16,'region'=32] {'region'}, dimensions={1} | all-to-all | bytes 524288 | tf_op jit(solution)/shard_map/all_to_all | solution.py:56
  127.8 23.3 %scatter_custom_fusion.1 = f32[16,1024]{0,1:T(8,128)} fusion(s32[4096]{0:T(1024)} %bitcast.173, f32[4096,16]{1,0:T(8,128)S(1)} %copy.49, f32[]{:T(128)} %constant.41.clone.1), kind=kCustom, calls=%fused_computation.111 | custom fusion | flops 65536 | bytes 66048 | tf_op jit(solution)/shard_map/scatter-add | solution.py:58
  151.0 108.9 %all-reduce.2.cloned.1.call-done = f32[16,1024]{0,1:T(8,128)} async-done(((f32[16,1024]{0,1:T(8,128)}), f32[16,1024]{0,1:T(8,128)}) %all-reduce.2.cloned.1.call-update) | async-done | bytes 65552 | tf_op jit(solution)/shard_map/psum | solution.py:60
  259.9 1.8 copy.50
  (55 shorter events, 11.1 us)
Async XLA Ops:
  6.5 45.5 %copy-start.1 = (f32[1024,256]{1,0:T(8,128)S(1)}, f32[1024,256]{1,0:T(8,128)}, u32[]{:S(2)}) copy-start(f32[1024,256]{1,0:T(8,128)} %param.13) | copy-start | bytes 3145732
  6.5 26.7 %all-to-all-start = ((s32[1,32,128]{2,0,1:T(1,128)}), s32[1,32,128]{2,0,1:T(1,128)S(1)}, u32[]{:S(2)}, u32[]{:S(2)}) async-start(s32[1,32,128]{2,0,1:T(1,128)} %bitcast.180), calls=%async_computation | async-start | bytes 32768 | tf_op jit(solution)/shard_map/all_to_all | solution.py:30
  33.2 0.6 copy-start.5
  46.3 5.9 %copy-start.2 = (f32[8,256]{1,0:T(8,128)S(1)}, f32[8,256]{1,0:T(8,128)}, u32[]{:S(2)}) copy-start(f32[8,256]{1,0:T(8,128)} %param.10) | copy-start | bytes 24580
  46.3 5.9 %copy-start.6 = (s32[8,256]{1,0:T(8,128)S(1)}, s32[8,256]{1,0:T(8,128)}, u32[]{:S(2)}) copy-start(s32[8,256]{1,0:T(8,128)} %param.11) | copy-start | bytes 24580
  47.0 21.1 %all-to-all-start.1 = ((bf16[16,32,128]{2,0,1:T(8,128)(2,1)}), bf16[16,32,128]{2,0,1:T(8,128)(2,1)S(1)}, u32[]{:S(2)}, u32[]{:S(2)}) async-start(bf16[16,32,128]{2,0,1:T(8,128)(2,1)} %broadcast_select_fusion.3), calls=%async_computation.1 | async-start | bytes 262144 | tf_op jit(solution)/shard_map/all_to_all | solution.py:35
  52.0 207.9 %all-reduce.2.cloned.1.call-start = ((), (), s32[]{:S(2)}) async-start(), calls=%async_computation.3 | async-start | bytes 1048576 | tf_op jit(solution)/shard_map/psum | solution.py:60
  52.3 2.4 copy-start.7
  75.9 2.4 copy-start.4
  75.9 2.4 copy-start.8
  83.0 1.0 copy-start
  84.0 2.6 copy-start.3
Sparse Core Ops, SparseCore 0:
  151.2 108.6 all-reduce.1
where the time goes:
time: 269 us
  waiting for transfers between devices  131 us (49%)
  other arithmetic  37.5 us (14%)
  local copies, waits for them, and re-layouts  33.9 us (13%)
  blocking collectives  25.2 us (9%)
  starting transfers between devices  20.5 us (8%)
  between operations  13.8 us (5%)
  matrix products  7.06 us (3%)
    psum x1, waiting for transfers between devices, on_device(): partial_value = lax.psum(partial_value, 'band')  109 us
    all_to_all x1, blocking collectives, on_device(): lax.all_to_all(sending, 'region', split_axis=1, concat_axis=1, tiled=True)  25.2 us
    scatter-add x1, other arithmetic, on_device(): jnp.zeros((state_count, state.shape[1]), jnp.float32).at[:, wanted]  23.3 us
    all_to_all x1, starting transfers between devices, on_device(): lax.all_to_all(request_rows, 'region', split_axis=1, concat_axis=0, tiled...  15.5 us
    all_to_all x1, waiting for transfers between devices, on_device(): lax.all_to_all(picked, 'region', split_axis=1, concat_axis=1, tiled=True)  12.8 us
    gather x2, local copies, waits for them, and re-layouts, on_device(): picked = jnp.take(state, wanted, axis=1)  12.5 us
    all_to_all x1, waiting for transfers between devices, on_device(): lax.all_to_all(request_rows, 'region', split_axis=1, concat_axis=0, tiled...  8.92 us
    gather x1, local copies, waits for them, and re-layouts, on_device(): state_x = jnp.take(arrived, slot_ids, axis=1)  7.34 us
  transfers between devices with their start and end apart: 3, of which 3 were waited for; matrix products, arithmetic and copies ran while one was open for 2% of the time, Pallas kernels for 0%

commit v1 on v0

v1 whole, which is shorter than its diff:
```python
import math

import jax
import jax.numpy as jnp
import ml_dtypes
from jax import lax
from jax.experimental import pallas as pl
from jax.experimental.pallas import tpu as pltpu
from jax.sharding import PartitionSpec as P

NS = 16
BINS = 1024
LEN = 8
RAYS = 256
CROSS = LEN * RAYS
OWNERS = 32
CAP = 128
BANDS = 16
KX = 128
BLOCK = 256
SUB = 16
LOG2E = 1.0 / math.log(2.0)
LN2 = math.log(2.0)
VMEM_LIMIT = 48 << 20

f32 = jnp.float32
bf16 = jnp.bfloat16


def three_parts(x):
    high = x.astype(bf16).astype(f32)
    mid = (x - high).astype(bf16).astype(f32)
    low = (x - high - mid).astype(bf16).astype(f32)
    return high, mid, low


def prepare_kernel(
    slot_ref, rows_ref, len_ref, wa_ref, we_ref, slot_hot_ref, low_hot_ref, high_ref, tag_ref, ext_ref, w_ref
):
    rows = rows_ref[...]
    row_low = (rows & 127).astype(f32)
    row_high = (rows >> 7).astype(f32)
    listed = jnp.concatenate([row_low, row_high], axis=0).astype(bf16)
    for owner in range(OWNERS):
        line = lax.broadcasted_iota(jnp.int32, (8, CAP), 0)
        tag_ref[owner] = jnp.where(
            line == 0, row_low[owner : owner + 1], jnp.where(line == 1, row_high[owner : owner + 1], 0.0)
        ).astype(bf16)
    lines = lax.broadcasted_iota(jnp.int32, (128, RAYS), 0)
    owner_lines = lax.broadcasted_iota(jnp.int32, (OWNERS, RAYS), 0)
    ext_lines = lax.broadcasted_iota(jnp.int32, (16, RAYS), 0)
    for j in range(LEN):
        cols = slice(j * RAYS, (j + 1) * RAYS)
        slot = slot_ref[j : j + 1, :]
        owner = slot >> 7
        slot_hot = jnp.where(lines == (slot & 127), 1.0, 0.0).astype(bf16)
        slot_hot_ref[:, cols] = slot_hot
        found = jnp.dot(listed, slot_hot, preferred_element_type=f32)
        mine = owner_lines == owner
        low = jnp.sum(jnp.where(mine, found[:OWNERS], 0.0), axis=0, keepdims=True)
        high = jnp.sum(jnp.where(mine, found[OWNERS:], 0.0), axis=0, keepdims=True)
        low_hot_ref[:, cols] = jnp.where(lines == low.astype(jnp.int32), 1.0, 0.0).astype(bf16)
        high_ref[j : j + 1, :] = owner * 8 + high.astype(jnp.int32)
        l0, l1, l2 = three_parts(jnp.log(len_ref[j : j + 1, :]) * LOG2E)
        ext_ref[:, cols] = jnp.where(
            ext_lines == 0,
            l0,
            jnp.where(ext_lines == 1, l1, jnp.where(ext_lines == 2, l2, jnp.where(ext_lines < 6, 1.0, 0.0))),
        ).astype(bf16)
    consts = []
    rest = math.log2(LOG2E)
    for _ in range(3):
        part = float(ml_dtypes.bfloat16(rest))
        consts.append(part)
        rest -= part
    step = 128
    tail = lax.broadcasted_iota(jnp.int32, (KX - 2 * NS, step), 0)
    for which, ref in ((0, wa_ref), (1, we_ref)):
        c0, c1, c2 = consts if which == 0 else (0.0, 0.0, 0.0)
        extra = jnp.where(
            tail < 3,
            1.0,
            jnp.where(tail == 3, c0, jnp.where(tail == 4, c1, jnp.where(tail == 5, c2, 0.0))),
        )
        for first in range(0, BINS, step):
            scaled = ref[:, first : first + step].astype(f32) * LOG2E
            high = scaled.astype(bf16).astype(f32)
            stacked = jnp.concatenate([high, scaled - high, extra], axis=0)
            w_ref[which, first : first + step, :] = stacked.T.astype(bf16)


def gather_kernel(table_ref, low_hot_ref, high_ref, out_ref, row_ref):
    table = table_ref[...].reshape(OWNERS * 8, 128)
    lines = lax.broadcasted_iota(jnp.int32, (OWNERS * 8, RAYS), 0)
    for j in range(LEN):
        found = jnp.dot(table, low_hot_ref[:, j * RAYS : (j + 1) * RAYS], preferred_element_type=f32)
        mine = lines == high_ref[j : j + 1, :]
        value = jnp.sum(jnp.where(mine, found, 0.0), axis=0, keepdims=True)
        row_ref[2 * j : 2 * j + 1, :] = value[:, :128]
        row_ref[2 * j + 1 : 2 * j + 2, :] = value[:, 128:]
    value = row_ref[...].astype(bf16)
    for peer in range(BANDS):
        out_ref[peer] = value


def adjoint_kernel(
    states_ref,
    ext_ref,
    w_ref,
    wa_ref,
    we_ref,
    slot_ref,
    slot_hot_ref,
    tag_ref,
    cot_ref,
    out_ref,
    x_ref,
    la_ref,
    le_ref,
    ga_ref,
    ge_ref,
    sum_a_ref,
    sum_e_ref,
    spread_ref,
):
    step = pl.program_id(0)

    @pl.when(step == 0)
    def _():
        for tile in range(CROSS // 128):
            cols = slice(tile * 128, (tile + 1) * 128)
            x = states_ref[:, tile, :]
            x_ref[0:NS, cols] = x
            x_ref[NS : 2 * NS, cols] = x
        x_ref[2 * NS : 3 * NS, :] = ext_ref[...]
        x_ref[3 * NS :, :] = jnp.zeros((KX - 3 * NS, CROSS), bf16)
        sum_a_ref[...] = jnp.zeros_like(sum_a_ref)
        sum_e_ref[...] = jnp.zeros_like(sum_e_ref)

    la_ref[...] = jnp.dot(w_ref[0], x_ref[...], preferred_element_type=f32)
    le_ref[...] = jnp.dot(w_ref[1], x_ref[...], preferred_element_type=f32)
    for first in range(0, BLOCK, SUB):
        bins = slice(first, first + SUB)
        for half in range(2):
            cot = cot_ref[bins, half * 128 : (half + 1) * 128]
            depths, emitteds = [], []
            passed = jnp.zeros((SUB, 128), f32)
            for j in range(LEN):
                cols = slice(j * RAYS + half * 128, j * RAYS + half * 128 + 128)
                depth = jnp.exp2(la_ref[bins, cols])
                emitteds.append(cot * jnp.exp2(le_ref[bins, cols] - passed))
                depths.append(depth)
                passed = passed + depth
            behind = jnp.zeros((SUB, 128), f32)
            for j in reversed(range(LEN)):
                cols = slice(j * RAYS + half * 128, j * RAYS + half * 128 + 128)
                ge_ref[bins, cols] = emitteds[j].astype(bf16)
                ga_ref[bins, cols] = (depths[j] * behind).astype(bf16)
                behind = behind + emitteds[j]
    sum_a_ref[...] += jnp.dot(wa_ref[...], ga_ref[...], preferred_element_type=f32)
    sum_e_ref[...] += jnp.dot(we_ref[...], ge_ref[...], preferred_element_type=f32)

    @pl.when(step == pl.num_programs(0) - 1)
    def _():
        for j in range(LEN):
            cols = slice(j * RAYS, (j + 1) * RAYS)
            value = sum_e_ref[:, cols] - LN2 * sum_a_ref[:, cols]
            owner = slot_ref[j : j + 1, :] >> 7
            for p in range(OWNERS):
                spread_ref[p * NS : (p + 1) * NS, cols] = jnp.where(owner == p, value, 0.0).astype(bf16)
        placed = lax.dot_general(
            spread_ref[...], slot_hot_ref[...], (((1,), (1,)), ((), ())), preferred_element_type=f32
        )
        for p in range(OWNERS):
            out_ref[p, 0:NS, :] = placed[p * NS : (p + 1) * NS].astype(bf16)
            out_ref[p, NS : NS + 8, :] = tag_ref[p]


def scatter_kernel(got_ref, out_ref, value_ref, low_hot_ref):
    lines = lax.broadcasted_iota(jnp.int32, (128, CAP), 0)
    for q in range(OWNERS):
        cols = slice(q * CAP, (q + 1) * CAP)
        value = got_ref[q, 0:NS, :].astype(f32)
        tags = got_ref[q, NS : NS + 8, :].astype(f32)
        low = tags[0:1, :].astype(jnp.int32)
        high = tags[1:2, :].astype(jnp.int32)
        low_hot_ref[:, cols] = jnp.where(lines == low, 1.0, 0.0).astype(bf16)
        for h in range(8):
            value_ref[h * NS : (h + 1) * NS, cols] = jnp.where(high == h, value, 0.0).astype(bf16)
    total = lax.dot_general(
        value_ref[...], low_hot_ref[...], (((1,), (1,)), ((), ())), preferred_element_type=f32
    )
    for h in range(8):
        part = total[h * NS : (h + 1) * NS].astype(bf16)
        for peer in range(BANDS):
            out_ref[peer, :, h * 128 : (h + 1) * 128] = part


def sum_kernel(part_ref, out_ref):
    total = part_ref[0].astype(f32)
    for peer in range(1, BANDS):
        total = total + part_ref[peer].astype(f32)
    out_ref[...] = total


def shape(dims, dtype):
    return jax.ShapeDtypeStruct(dims, dtype)


PARAMS = pltpu.CompilerParams(vmem_limit_bytes=VMEM_LIMIT)


def on_device(
    state, absorb_weight, emit_weight, path_len, crossing_slot, request_rows, cot_intensity
):
    band = lax.axis_index("band")
    mine = lax.dynamic_slice_in_dim(state, band, 1, axis=0).reshape(1, 8, 128)
    table = lax.all_to_all(
        jnp.broadcast_to(mine, (OWNERS, 8, 128)), "region", split_axis=0, concat_axis=0, tiled=True
    )
    slot_hot, low_hot, high, tags, ext, weights = pl.pallas_call(
        prepare_kernel,
        out_shape=(
            shape((128, CROSS), bf16),
            shape((128, CROSS), bf16),
            shape((LEN, RAYS), jnp.int32),
            shape((OWNERS, 8, CAP), bf16),
            shape((NS, CROSS), bf16),
            shape((2, BINS, KX), bf16),
        ),
        compiler_params=PARAMS,
        cost_estimate=pl.CostEstimate(flops=40_000_000, bytes_accessed=2_000_000, transcendentals=4096),
    )(crossing_slot, request_rows.reshape(OWNERS, CAP), path_len, absorb_weight, emit_weight)
    picked = pl.pallas_call(
        gather_kernel,
        out_shape=shape((BANDS, NS, 128), bf16),
        scratch_shapes=[pltpu.VMEM((CROSS // 128, 128), f32)],
        compiler_params=PARAMS,
    )(table, low_hot, high)
    states = lax.all_to_all(picked, "band", split_axis=0, concat_axis=0, tiled=True)
    whole = lambda *dims: pl.BlockSpec(dims, lambda i: (0,) * len(dims))
    sending = pl.pallas_call(
        adjoint_kernel,
        grid=(BINS // BLOCK,),
        in_specs=[
            whole(NS, CROSS // 128, 128),
            whole(NS, CROSS),
            pl.BlockSpec((2, BLOCK, KX), lambda i: (0, i, 0)),
            pl.BlockSpec((NS, BLOCK), lambda i: (0, i)),
            pl.BlockSpec((NS, BLOCK), lambda i: (0, i)),
            whole(LEN, RAYS),
            whole(128, CROSS),
            whole(OWNERS, 8, CAP),
            pl.BlockSpec((BLOCK, RAYS), lambda i: (i, 0)),
        ],
        out_specs=whole(OWNERS, NS + 8, CAP),
        out_shape=shape((OWNERS, NS + 8, CAP), bf16),
        scratch_shapes=[
            pltpu.VMEM((KX, CROSS), bf16),
            pltpu.VMEM((BLOCK, CROSS), f32),
            pltpu.VMEM((BLOCK, CROSS), f32),
            pltpu.VMEM((BLOCK, CROSS), bf16),
            pltpu.VMEM((BLOCK, CROSS), bf16),
            pltpu.VMEM((NS, CROSS), f32),
            pltpu.VMEM((NS, CROSS), f32),
            pltpu.VMEM((OWNERS * NS, CROSS), bf16),
        ],
        compiler_params=PARAMS,
    )(
        states,
        ext,
        weights,
        absorb_weight,
        emit_weight,
        crossing_slot,
        slot_hot,
        tags,
        cot_intensity,
    )
    returned = lax.all_to_all(sending, "region", split_axis=0, concat_axis=0, tiled=True)
    partial = pl.pallas_call(
        scatter_kernel,
        out_shape=shape((BANDS, NS, 1024), bf16),
        scratch_shapes=[pltpu.VMEM((128, OWNERS * CAP), bf16), pltpu.VMEM((128, OWNERS * CAP), bf16)],
        compiler_params=PARAMS,
    )(returned)
    parts = lax.all_to_all(partial, "band", split_axis=0, concat_axis=0, tiled=True)
    return pl.pallas_call(
        sum_kernel, out_shape=shape((NS, 1024), f32), compiler_params=PARAMS
    )(parts)


def solution(mesh):
    return jax.shard_map(
        on_device,
        mesh=mesh,
        in_specs=(
            P(None, "region"),
            P(None, "band"),
            P(None, "band"),
            P(None, "region"),
            P(None, "region"),
            P("region", None, None),
            P("band", "region"),
        ),
        out_specs=P(None, "region"),
        check_vma=False,
    )
```

time: 269 us -> 90.9 us (0.34)
  the two profiles are of different devices: /device:TPU:32 before, /device:TPU:8 now
where the time goes in v1:
time: 90.9 us; the launch traced here: 90.3 us
  blocking collectives  50.5 us (56%)
  starting transfers between devices  15.5 us (17%)
  waiting for transfers between devices  10.2 us (11%)
  Pallas kernels  8.97 us (10%)
  local copies, waits for them, and re-layouts  5.07 us (6%)
    all_to_all x1, blocking collectives, on_device(): lax.all_to_all(sending, 'region', split_axis=0, concat_axis=0, tiled=True)  23 us
    all_to_all x1, starting transfers between devices, on_device(): lax.all_to_all(jnp.broadcast_to(mine, (OWNERS, 8, 128)), 'region', split_...  15.5 us
    all_to_all x1, blocking collectives, on_device(): lax.all_to_all(partial, 'band', split_axis=0, concat_axis=0, tiled=True)  13.9 us
    all_to_all x1, blocking collectives, on_device(): lax.all_to_all(picked, 'band', split_axis=0, concat_axis=0, tiled=True)  13.6 us
    all_to_all x1, waiting for transfers between devices, on_device(): lax.all_to_all(jnp.broadcast_to(mine, (OWNERS, 8, 128)), 'region', split_...  10.2 us
    pallas_call x1, Pallas kernels, on_device(): pl.pallas_call(adjoint_kernel, grid=(BINS // BLOCK,), in_specs=[whole(NS,...  6.32 us
    unnamed x20, local copies, waits for them, and re-layouts  4.4 us
  transfers between devices with their start and end apart: 1, of which 1 were waited for; matrix products, arithmetic and copies ran while one was open for 0% of the time, Pallas kernels for 1%

profile of v1, /device:TPU:8, one launch (start us, length us, event | category | flops | bytes accessed | tf_op | source)
XLA Modules:
  0.0 90.3 jit_solution(1165976551992764711)
XLA Ops:
  0.0 0.0 copy-start
  0.0 0.8 copy-done
  0.8 0.6 broadcast_in_dim.8
  1.4 15.5 %all-to-all-start = ((bf16[32,8,128]{2,1,0:T(8,128)(2,1)}), bf16[32,8,128]{2,1,0:T(8,128)(2,1)S(1)}, u32[]{:S(2)}, u32[]{:S(2)}) async-start(bf16[32,8,128]{2,1,0:T(8,128)(2,1)} %broadcast_in_dim.8), calls=%async_computation | async-start | bytes 131072 | tf_op jit(solution)/shard_map/all_to_all | solution.py:218
  16.9 0.0 copy-start.2
  16.9 0.7 copy-done.2
  17.7 0.8 copy-done.4
  18.4 0.7 copy-done.6
  19.1 0.7 copy-done.8
  19.9 0.7 copy-done.9
  20.6 0.5 shard_map.73
  21.1 10.2 %all-to-all-done.table_ref = bf16[32,8,128]{2,1,0:T(8,128)(2,1)S(1)} async-done(((bf16[32,8,128]{2,1,0:T(8,128)(2,1)}), bf16[32,8,128]{2,1,0:T(8,128)(2,1)S(1)}, u32[]{:S(2)}, u32[]{:S(2)}) %all-to-all-start) | async-done | bytes 65568 | tf_op jit(solution)/shard_map/all_to_all | solution.py:218
  31.3 0.4 shard_map.74
  31.8 0.0 copy-start.3
  31.8 0.0 copy-start.5
  31.8 0.0 copy-start.7
  31.8 13.6 %all_to_all.20.states_ref = bf16[16,16,128]{2,1,0:T(8,128)(2,1)S(1)} all-to-all(bf16[16,16,128]{2,1,0:T(8,128)(2,1)S(1)} %shard_map.74), channel_id=1, replica_groups=mesh['band'=16,'region'=32] {'band'}, dimensions={0} | all-to-all | bytes 131072 | tf_op jit(solution)/shard_map/all_to_all | solution.py:240
  45.4 0.0 copy-done.1
  45.4 0.0 copy-done.7
  45.4 6.3 %shard_map.75 = bf16[32,24,128]{2,1,0:T(8,128)(2,1)S(1)} custom-call(bf16[16,16,128]{2,1,0:T(8,128)(2,1)S(1)} %all_to_all.20.states_ref, bf16[16,2048]{1,0:T(8,128)(2,1)S(1)} %get-tuple-element.13.ext_ref, bf16[2,1024,128]{2,1,0:T(8,128)(2,1)S(1)} %get-tuple-element.14.w_ref, bf16[16,1024]{1,0:T(8,128)(2,1)S(1)} %copy-done.3, ...), custom_call_target="tpu_custom_call" | custom-call | tf_op jit(solution)/shard_map/pallas_call | solution.py:242
  51.8 23.0 %all_to_all.21.got_ref = bf16[32,24,128]{2,1,0:T(8,128)(2,1)S(1)} all-to-all(bf16[32,24,128]{2,1,0:T(8,128)(2,1)S(1)} %shard_map.75), channel_id=1, replica_groups=mesh['band'=16,'region'=32] {'region'}, dimensions={0} | all-to-all | bytes 393216 | tf_op jit(solution)/shard_map/all_to_all | solution.py:280
  74.7 1.0 %shard_map.76 = bf16[16,16,1024]{2,1,0:T(8,128)(2,1)S(1)} custom-call(bf16[32,24,128]{2,1,0:T(8,128)(2,1)S(1)} %all_to_all.21.got_ref), custom_call_target="tpu_custom_call" | custom-call | tf_op jit(solution)/shard_map/pallas_call | solution.py:281
  75.7 13.9 %all_to_all.22.part_ref = bf16[16,16,1024]{2,1,0:T(8,128)(2,1)S(1)} all-to-all(bf16[16,16,1024]{2,1,0:T(8,128)(2,1)S(1)} %shard_map.76), channel_id=1, replica_groups=mesh['band'=16,'region'=32] {'band'}, dimensions={0} | all-to-all | bytes 1048576 | tf_op jit(solution)/shard_map/all_to_all | solution.py:287
  89.6 0.7 shard_map.77
  (8 shorter events, 0.0 us)
Async XLA Ops:
  0.0 0.8 copy-start
  0.0 45.4 %copy-start.1 = (f32[1024,256]{1,0:T(8,128)S(1)}, f32[1024,256]{1,0:T(8,128)}, u32[]{:S(2)}) copy-start(f32[1024,256]{1,0:T(8,128)} %cot_ref.1) | copy-start | bytes 3145732
  1.4 29.9 %all-to-all-start = ((bf16[32,8,128]{2,1,0:T(8,128)(2,1)}), bf16[32,8,128]{2,1,0:T(8,128)(2,1)S(1)}, u32[]{:S(2)}, u32[]{:S(2)}) async-start(bf16[32,8,128]{2,1,0:T(8,128)(2,1)} %broadcast_in_dim.8), calls=%async_computation | async-start | bytes 131072 | tf_op jit(solution)/shard_map/all_to_all | solution.py:218
  16.9 0.8 copy-start.2
  17.7 0.8 copy-start.4
  18.4 0.7 copy-start.6
  19.1 0.7 copy-start.8
  19.9 0.7 copy-start.9
  31.8 13.7 %copy-start.3 = (bf16[16,1024]{1,0:T(8,128)(2,1)S(1)}, bf16[16,1024]{1,0:T(8,128)(2,1)}, u32[]{:S(2)}) copy-start(bf16[16,1024]{1,0:T(8,128)(2,1)} %wa_ref.3) | copy-start | bytes 98308
  31.8 13.7 %copy-start.5 = (bf16[16,1024]{1,0:T(8,128)(2,1)S(1)}, bf16[16,1024]{1,0:T(8,128)(2,1)}, u32[]{:S(2)}) copy-start(bf16[16,1024]{1,0:T(8,128)(2,1)} %we_ref.3) | copy-start | bytes 98308
  31.8 13.7 %copy-start.7 = (s32[8,256]{1,0:T(8,128)S(1)}, s32[8,256]{1,0:T(8,128)}, u32[]{:S(2)}) copy-start(s32[8,256]{1,0:T(8,128)} %slot_ref.3) | copy-start | bytes 24580

commit v2 on v1

v2 whole, which is shorter than its diff:
```python
import math

import jax
import jax.numpy as jnp
import ml_dtypes
from jax import lax
from jax.experimental import pallas as pl
from jax.experimental.pallas import tpu as pltpu
from jax.sharding import PartitionSpec as P

NS = 16
BINS = 1024
LEN = 8
RAYS = 256
CROSS = LEN * RAYS
OWNERS = 32
CAP = 128
BANDS = 16
KX = 48
KW = 128
BLOCK = 128
SUB = 16
LOG2E = 1.0 / math.log(2.0)
LN2 = math.log(2.0)
VMEM_LIMIT = 48 << 20

f32 = jnp.float32
bf16 = jnp.bfloat16


def three_parts(x):
    high = x.astype(bf16).astype(f32)
    mid = (x - high).astype(bf16).astype(f32)
    low = (x - high - mid).astype(bf16).astype(f32)
    return high, mid, low


def component_kernel(state_ref, out_ref):
    band = lax.axis_index("band")
    mine = lax.broadcasted_iota(jnp.int32, (NS, 128), 0) == band
    rows = []
    for h in range(8):
        part = state_ref[:, h * 128 : (h + 1) * 128].astype(f32)
        rows.append(jnp.sum(jnp.where(mine, part, 0.0), axis=0, keepdims=True))
    value = jnp.concatenate(rows, axis=0).astype(bf16)
    for region in range(OWNERS):
        out_ref[region] = value


def prepare_kernel(
    slot_ref, rows_ref, len_ref, wa_ref, we_ref, slot_hot_ref, low_hot_ref, high_ref, tag_ref, ext_ref, w_ref
):
    rows = rows_ref[...]
    row_low = (rows & 127).astype(f32)
    row_high = (rows >> 7).astype(f32)
    listed = jnp.concatenate([row_low, row_high], axis=0).astype(bf16)
    for owner in range(OWNERS):
        tag_ref[owner] = jnp.concatenate(
            [row_low[owner : owner + 1], row_high[owner : owner + 1]], axis=0
        ).astype(bf16)
    lines = lax.broadcasted_iota(jnp.int32, (128, RAYS), 0)
    wide_lines = lax.broadcasted_iota(jnp.int32, (2 * CAP, RAYS), 0)
    owner_lines = lax.broadcasted_iota(jnp.int32, (OWNERS, RAYS), 0)
    ext_lines = lax.broadcasted_iota(jnp.int32, (16, RAYS), 0)
    for j in range(LEN):
        cols = slice(j * RAYS, (j + 1) * RAYS)
        slot = slot_ref[j : j + 1, :]
        owner = slot >> 7
        slot_hot = jnp.where(lines == (slot & 127), 1.0, 0.0).astype(bf16)
        slot_hot_ref[:, cols] = jnp.where(wide_lines == (slot & 255), 1.0, 0.0).astype(bf16)
        found = jnp.dot(listed, slot_hot, preferred_element_type=f32)
        mine = owner_lines == owner
        low = jnp.sum(jnp.where(mine, found[:OWNERS], 0.0), axis=0, keepdims=True)
        high = jnp.sum(jnp.where(mine, found[OWNERS:], 0.0), axis=0, keepdims=True)
        low_hot_ref[:, cols] = jnp.where(lines == low.astype(jnp.int32), 1.0, 0.0).astype(bf16)
        high_ref[j : j + 1, :] = owner * 8 + high.astype(jnp.int32)
        l0, l1, l2 = three_parts(jnp.log(len_ref[j : j + 1, :]) * LOG2E)
        ext_ref[:, cols] = jnp.where(
            ext_lines == 0,
            l0,
            jnp.where(ext_lines == 1, l1, jnp.where(ext_lines == 2, l2, jnp.where(ext_lines < 6, 1.0, 0.0))),
        ).astype(bf16)
    consts = []
    rest = math.log2(LOG2E)
    for _ in range(3):
        part = float(ml_dtypes.bfloat16(rest))
        consts.append(part)
        rest -= part
    step = 128
    tail = lax.broadcasted_iota(jnp.int32, (KW - 2 * NS, step), 0)
    for which, ref in ((0, wa_ref), (1, we_ref)):
        c0, c1, c2 = consts if which == 0 else (0.0, 0.0, 0.0)
        extra = jnp.where(
            tail < 3,
            1.0,
            jnp.where(tail == 3, c0, jnp.where(tail == 4, c1, jnp.where(tail == 5, c2, 0.0))),
        )
        for first in range(0, BINS, step):
            scaled = ref[:, first : first + step].astype(f32) * LOG2E
            high = scaled.astype(bf16).astype(f32)
            stacked = jnp.concatenate([high, scaled - high, extra], axis=0)
            w_ref[which, first : first + step, :] = stacked.T.astype(bf16)


def gather_kernel(table_ref, low_hot_ref, high_ref, out_ref, row_ref):
    table = table_ref[...].reshape(OWNERS * 8, 128)
    lines = lax.broadcasted_iota(jnp.int32, (OWNERS * 8, RAYS), 0)
    for j in range(LEN):
        found = jnp.dot(table, low_hot_ref[:, j * RAYS : (j + 1) * RAYS], preferred_element_type=f32)
        mine = lines == high_ref[j : j + 1, :]
        value = jnp.sum(jnp.where(mine, found, 0.0), axis=0, keepdims=True)
        row_ref[2 * j : 2 * j + 1, :] = value[:, :128]
        row_ref[2 * j + 1 : 2 * j + 2, :] = value[:, 128:]
    value = row_ref[...].astype(bf16)
    for peer in range(BANDS):
        out_ref[peer] = value


def adjoint_kernel(
    states_ref,
    ext_ref,
    w_ref,
    wa_ref,
    we_ref,
    slot_ref,
    slot_hot_ref,
    tag_ref,
    cot_ref,
    out_ref,
    x_ref,
    la0_ref,
    la1_ref,
    le0_ref,
    le1_ref,
    ga0_ref,
    ga1_ref,
    ge0_ref,
    ge1_ref,
    sum_a_ref,
    sum_e_ref,
    spread_ref,
):
    la_refs, le_refs = (la0_ref, la1_ref), (le0_ref, le1_ref)
    ga_refs, ge_refs = (ga0_ref, ga1_ref), (ge0_ref, ge1_ref)
    blocks = BINS // BLOCK
    for tile in range(CROSS // 128):
        cols = slice(tile * 128, (tile + 1) * 128)
        x = states_ref[:, tile, :]
        x_ref[0:NS, cols] = x
        x_ref[NS : 2 * NS, cols] = x
    x_ref[2 * NS : 3 * NS, :] = ext_ref[...]

    def logits(block, j):
        bins = slice(block * BLOCK, (block + 1) * BLOCK)
        cols = slice(j * RAYS, (j + 1) * RAYS)
        x = x_ref[:, cols]
        if j < LEN - 1:
            la_refs[block % 2][:, cols] = jnp.dot(w_ref[0, bins, :KX], x, preferred_element_type=f32)
        le_refs[block % 2][:, cols] = jnp.dot(w_ref[1, bins, :KX], x, preferred_element_type=f32)

    def contract(block, j):
        bins = slice(block * BLOCK, (block + 1) * BLOCK)
        cols = slice(j * RAYS, (j + 1) * RAYS)
        for w, g_refs, sum_ref in ((wa_ref, ga_refs, sum_a_ref), (we_ref, ge_refs, sum_e_ref)):
            if w is wa_ref and j == LEN - 1:
                continue
            part = jnp.dot(w[:, bins], g_refs[block % 2][:, cols], preferred_element_type=f32)
            sum_ref[:, cols] = part if block == 0 else sum_ref[:, cols] + part

    def adjoint(block, first, half):
        la_ref, le_ref = la_refs[block % 2], le_refs[block % 2]
        ga_ref, ge_ref = ga_refs[block % 2], ge_refs[block % 2]
        bins = slice(first, first + SUB)
        cot = cot_ref[block * BLOCK + first : block * BLOCK + first + SUB, half * 128 : (half + 1) * 128]
        depths, emitteds = [], []
        passed = None
        for j in range(LEN):
            cols = slice(j * RAYS + half * 128, j * RAYS + half * 128 + 128)
            power = le_ref[bins, cols]
            emitteds.append(cot * jnp.exp2(power if passed is None else power - passed))
            if j < LEN - 1:
                depth = jnp.exp2(la_ref[bins, cols])
                depths.append(depth)
                passed = depth if passed is None else passed + depth
        behind = None
        for j in reversed(range(LEN)):
            cols = slice(j * RAYS + half * 128, j * RAYS + half * 128 + 128)
            ge_ref[bins, cols] = emitteds[j].astype(bf16)
            if behind is None:
                behind = emitteds[j]
            else:
                ga_ref[bins, cols] = (depths[j] * behind).astype(bf16)
                behind = behind + emitteds[j]

    for j in range(LEN):
        logits(0, j)
    for block in range(blocks):
        units = [(first, half) for first in range(0, BLOCK, SUB) for half in range(2)]
        matmuls = []
        for j in range(LEN):
            if block + 1 < blocks:
                matmuls.append((logits, block + 1, j))
            if block > 0:
                matmuls.append((contract, block - 1, j))
        done = 0
        for index, (first, half) in enumerate(units):
            while done * len(units) < len(matmuls) * (index + 1) and done < len(matmuls):
                f, which, j = matmuls[done]
                f(which, j)
                done += 1
            adjoint(block, first, half)
    for j in range(LEN):
        contract(blocks - 1, j)

    for j in range(LEN):
        cols = slice(j * RAYS, (j + 1) * RAYS)
        value = sum_e_ref[:, cols]
        if j < LEN - 1:
            value = value - LN2 * sum_a_ref[:, cols]
        pair = slot_ref[j : j + 1, :] >> 8
        for p in range(OWNERS // 2):
            spread_ref[p * NS : (p + 1) * NS, cols] = jnp.where(pair == p, value, 0.0).astype(bf16)
    placed = lax.dot_general(
        spread_ref[...], slot_hot_ref[...], (((1,), (1,)), ((), ())), preferred_element_type=f32
    ).astype(bf16)
    for p in range(OWNERS):
        rows = slice((p // 2) * NS, (p // 2 + 1) * NS)
        mine = placed[rows, (p % 2) * CAP : (p % 2 + 1) * CAP]
        out_ref[9 * p : 9 * p + 8] = mine.reshape(NS // 2, 2, CAP)
        out_ref[9 * p + 8] = tag_ref[p]


def scatter_kernel(got_ref, out_ref, value_ref, low_hot_ref):
    lines = lax.broadcasted_iota(jnp.int32, (128, CAP), 0)
    for q in range(OWNERS):
        cols = slice(q * CAP, (q + 1) * CAP)
        value = got_ref[9 * q : 9 * q + 8].reshape(NS, CAP).astype(f32)
        tags = got_ref[9 * q + 8].astype(f32)
        low = tags[0:1, :].astype(jnp.int32)
        high = tags[1:2, :].astype(jnp.int32)
        low_hot_ref[:, cols] = jnp.where(lines == low, 1.0, 0.0).astype(bf16)
        for h in range(8):
            value_ref[h * NS : (h + 1) * NS, cols] = jnp.where(high == h, value, 0.0).astype(bf16)
    total = lax.dot_general(
        value_ref[...], low_hot_ref[...], (((1,), (1,)), ((), ())), preferred_element_type=f32
    )
    for h in range(8):
        part = total[h * NS : (h + 1) * NS].astype(bf16)
        for peer in range(BANDS):
            out_ref[peer, :, h * 128 : (h + 1) * 128] = part


def sum_kernel(part_ref, out_ref):
    total = part_ref[0].astype(f32)
    for peer in range(1, BANDS):
        total = total + part_ref[peer].astype(f32)
    out_ref[...] = total


def shape(dims, dtype):
    return jax.ShapeDtypeStruct(dims, dtype)


PARAMS = pltpu.CompilerParams(vmem_limit_bytes=VMEM_LIMIT)


def call(kernel, out_shape, **kwargs):
    return pl.pallas_call(kernel, out_shape=out_shape, compiler_params=PARAMS, **kwargs)


def prepare(crossing_slot, rows, path_len, absorb_weight, emit_weight):
    return call(
        prepare_kernel,
        (
            shape((2 * CAP, CROSS), bf16),
            shape((128, CROSS), bf16),
            shape((LEN, RAYS), jnp.int32),
            shape((OWNERS, 2, CAP), bf16),
            shape((NS, CROSS), bf16),
            shape((2, BINS, KW), bf16),
        ),
        cost_estimate=pl.CostEstimate(flops=40_000_000, bytes_accessed=2_000_000, transcendentals=4096),
    )(crossing_slot, rows, path_len, absorb_weight, emit_weight)


def adjoint(states, prepared, absorb_weight, emit_weight, crossing_slot, cot_intensity):
    slot_hot, _, _, tags, ext, weights = prepared
    return call(
        adjoint_kernel,
        shape((OWNERS * 9, 2, CAP), bf16),
        scratch_shapes=[pltpu.VMEM((KX, CROSS), bf16)]
        + [pltpu.VMEM((BLOCK, CROSS), f32)] * 4
        + [pltpu.VMEM((BLOCK, CROSS), bf16)] * 4
        + [pltpu.VMEM((NS, CROSS), f32)] * 2
        + [pltpu.VMEM((OWNERS // 2 * NS, CROSS), bf16)],
    )(
        states,
        ext,
        weights,
        absorb_weight,
        emit_weight,
        crossing_slot,
        slot_hot,
        tags,
        cot_intensity,
    )


def on_device(
    state, absorb_weight, emit_weight, path_len, crossing_slot, request_rows, cot_intensity
):
    component = call(component_kernel, shape((OWNERS, 8, 128), bf16))(state)
    table = lax.all_to_all(component, "region", split_axis=0, concat_axis=0, tiled=True)
    prepared = prepare(
        crossing_slot, request_rows.reshape(OWNERS, CAP), path_len, absorb_weight, emit_weight
    )
    picked = call(
        gather_kernel,
        shape((BANDS, NS, 128), bf16),
        scratch_shapes=[pltpu.VMEM((CROSS // 128, 128), f32)],
    )(table, prepared[1], prepared[2])
    states = lax.all_to_all(picked, "band", split_axis=0, concat_axis=0, tiled=True)
    sending = adjoint(states, prepared, absorb_weight, emit_weight, crossing_slot, cot_intensity)
    returned = lax.all_to_all(sending, "region", split_axis=0, concat_axis=0, tiled=True)
    partial = call(
        scatter_kernel,
        shape((BANDS, NS, 1024), bf16),
        scratch_shapes=[pltpu.VMEM((128, OWNERS * CAP), bf16), pltpu.VMEM((128, OWNERS * CAP), bf16)],
    )(returned)
    parts = lax.all_to_all(partial, "band", split_axis=0, concat_axis=0, tiled=True)
    return call(sum_kernel, shape((NS, 1024), f32))(parts)


def solution(mesh):
    return jax.shard_map(
        on_device,
        mesh=mesh,
        in_specs=(
            P(None, "region"),
            P(None, "band"),
            P(None, "band"),
            P(None, "region"),
            P(None, "region"),
            P("region", None, None),
            P("band", "region"),
        ),
        out_specs=P(None, "region"),
        check_vma=False,
    )
```

time: 90.9 us -> 87.1 us (0.958)
  blocking collectives: 50.5 us -> 48.6 us
    all_to_all x1, blocking collectives: 23 us -> 20.9 us  [on_device(): lax.all_to_all(sending, 'region', split_axis=0, concat_axis=0, tiled=True)]
    pallas_call x5 -> x6, Pallas kernels: 8.97 us -> 8.07 us  [the longest x1 4.3 us: adjoint(): call(adjoint_kernel, shape((OWNERS * 9, 2, CAP), bf16), scratch_shapes=[p...]
where the time goes in v2:
time: 87.1 us; the launch traced here: 86.4 us
  blocking collectives  48.6 us (56%)
  starting transfers between devices  15.5 us (18%)
  waiting for transfers between devices  9.83 us (11%)
  Pallas kernels  8.07 us (9%)
  local copies, waits for them, and re-layouts  4.4 us (5%)
    all_to_all x1, blocking collectives, on_device(): lax.all_to_all(sending, 'region', split_axis=0, concat_axis=0, tiled=True)  20.9 us
    all_to_all x1, starting transfers between devices, on_device(): lax.all_to_all(component, 'region', split_axis=0, concat_axis=0, tiled=True)  15.5 us
    all_to_all x1, blocking collectives, on_device(): lax.all_to_all(partial, 'band', split_axis=0, concat_axis=0, tiled=True)  14.1 us
    all_to_all x1, blocking collectives, on_device(): lax.all_to_all(picked, 'band', split_axis=0, concat_axis=0, tiled=True)  13.6 us
    all_to_all x1, waiting for transfers between devices, on_device(): lax.all_to_all(component, 'region', split_axis=0, concat_axis=0, tiled=True)  9.83 us
    unnamed x20, local copies, waits for them, and re-layouts  4.4 us
    pallas_call x1, Pallas kernels, adjoint(): call(adjoint_kernel, shape((OWNERS * 9, 2, CAP), bf16), scratch_shapes=[p...  4.3 us
  transfers between devices with their start and end apart: 1, of which 1 were waited for; matrix products, arithmetic and copies ran while one was open for 0% of the time, Pallas kernels for 1%

profile of v2, /device:TPU:8, one launch (start us, length us, event | category | flops | bytes accessed | tf_op | source)
XLA Modules:
  0.0 86.4 jit_solution(15524308052618703861)
XLA Ops:
  0.0 0.8 copy-done.5
  0.8 0.7 shard_map.73
  1.4 15.5 %all-to-all-start = ((bf16[32,8,128]{2,1,0:T(8,128)(2,1)}), bf16[32,8,128]{2,1,0:T(8,128)(2,1)S(1)}, u32[]{:S(2)}, u32[]{:S(2)}) async-start(bf16[32,8,128]{2,1,0:T(8,128)(2,1)} %shard_map.73), calls=%async_computation | async-start | bytes 131072 | tf_op jit(solution)/shard_map/all_to_all | solution.py:313
  16.9 0.0 copy-start.1
  16.9 0.7 copy-done.1
  17.7 0.8 copy-done.3
  18.4 0.7 copy-done.6
  19.1 0.7 copy-done.8
  19.8 0.7 copy-done.9
  20.5 0.9 %shard_map.74 = (bf16[256,2048]{1,0:T(8,128)(2,1)S(1)}, bf16[128,2048]{1,0:T(8,128)(2,1)S(1)}, s32[8,256]{1,0:T(8,128)S(1)}, bf16[32,2,128]{2,1,0:T(2,128)(2,1)S...) custom-call(s32[8,256]{1,0:T(8,128)S(1)} %copy-done.6, s32[32,128]{1,0:T(8,128)S(1)} %bitcast.1, ...), custom_call_target="tpu_custom_call" | custom-call | flops 40000000 | bytes 2000000 | tf_op jit(solution)/shard_map/pallas_call | solution.py:272
  21.5 9.8 %all-to-all-done.table_ref = bf16[32,8,128]{2,1,0:T(8,128)(2,1)S(1)} async-done(((bf16[32,8,128]{2,1,0:T(8,128)(2,1)}), bf16[32,8,128]{2,1,0:T(8,128)(2,1)S(1)}, u32[]{:S(2)}, u32[]{:S(2)}) %all-to-all-start) | async-done | bytes 65568 | tf_op jit(solution)/shard_map/all_to_all | solution.py:313
  31.3 0.4 shard_map.75
  31.7 0.0 copy-start.2
  31.8 0.0 copy-start.4
  31.8 0.0 copy-start.7
  31.8 13.6 %all_to_all.20.states_ref = bf16[16,16,128]{2,1,0:T(8,128)(2,1)S(1)} all-to-all(bf16[16,16,128]{2,1,0:T(8,128)(2,1)S(1)} %shard_map.75), channel_id=1, replica_groups=mesh['band'=16,'region'=32] {'band'}, dimensions={0} | all-to-all | bytes 131072 | tf_op jit(solution)/shard_map/all_to_all | solution.py:322
  45.4 0.0 copy-done
  45.4 0.0 copy-done.2
  45.4 0.0 copy-done.4
  45.4 4.3 %shard_map.76 = bf16[288,2,128]{2,1,0:T(2,128)(2,1)S(1)} custom-call(bf16[16,16,128]{2,1,0:T(8,128)(2,1)S(1)} %all_to_all.20.states_ref, bf16[16,2048]{1,0:T(8,128)(2,1)S(1)} %get-tuple-element.13.ext_ref, bf16[2,1024,128]{2,1,0:T(8,128)(2,1)S(1)} %get-tuple-element.14.w_ref, bf16[16,1024]{1,0:T(8,128)(2,1)S(1)} %copy-done.2, ...), custom_call_target="tpu_custom_call" | custom-call | tf_op jit(solution)/shard_map/pallas_call | solution.py:288
  49.7 20.9 %all_to_all.21.got_ref = bf16[288,2,128]{2,1,0:T(2,128)(2,1)S(1)} all-to-all(bf16[288,2,128]{2,1,0:T(2,128)(2,1)S(1)} %shard_map.76), channel_id=1, replica_groups=mesh['band'=16,'region'=32] {'region'}, dimensions={0} | all-to-all | bytes 294912 | tf_op jit(solution)/shard_map/all_to_all | solution.py:324
  70.6 1.0 %shard_map.77 = bf16[16,16,1024]{2,1,0:T(8,128)(2,1)S(1)} custom-call(bf16[288,2,128]{2,1,0:T(2,128)(2,1)S(1)} %all_to_all.21.got_ref), custom_call_target="tpu_custom_call" | custom-call | tf_op jit(solution)/shard_map/pallas_call | solution.py:325
  71.7 14.1 %all_to_all.22.part_ref = bf16[16,16,1024]{2,1,0:T(8,128)(2,1)S(1)} all-to-all(bf16[16,16,1024]{2,1,0:T(8,128)(2,1)S(1)} %shard_map.77), channel_id=1, replica_groups=mesh['band'=16,'region'=32] {'band'}, dimensions={0} | all-to-all | bytes 1048576 | tf_op jit(solution)/shard_map/all_to_all | solution.py:330
  85.7 0.7 shard_map.78
  (7 shorter events, 0.0 us)
Async XLA Ops:
  0.0 0.8 copy-start.5
  0.8 44.7 %copy-start = (f32[1024,256]{1,0:T(8,128)S(1)}, f32[1024,256]{1,0:T(8,128)}, u32[]{:S(2)}) copy-start(f32[1024,256]{1,0:T(8,128)} %cot_ref.1) | copy-start | bytes 3145732
  1.4 29.9 %all-to-all-start = ((bf16[32,8,128]{2,1,0:T(8,128)(2,1)}), bf16[32,8,128]{2,1,0:T(8,128)(2,1)S(1)}, u32[]{:S(2)}, u32[]{:S(2)}) async-start(bf16[32,8,128]{2,1,0:T(8,128)(2,1)} %shard_map.73), calls=%async_computation | async-start | bytes 131072 | tf_op jit(solution)/shard_map/all_to_all | solution.py:313
  16.9 0.8 copy-start.1
  17.7 0.8 copy-start.3
  18.4 0.7 copy-start.6
  19.1 0.7 copy-start.8
  19.8 0.7 copy-start.9
  31.7 13.7 %copy-start.2 = (bf16[16,1024]{1,0:T(8,128)(2,1)S(1)}, bf16[16,1024]{1,0:T(8,128)(2,1)}, u32[]{:S(2)}) copy-start(bf16[16,1024]{1,0:T(8,128)(2,1)} %wa_ref.3) | copy-start | bytes 98308
  31.8 13.7 %copy-start.4 = (bf16[16,1024]{1,0:T(8,128)(2,1)S(1)}, bf16[16,1024]{1,0:T(8,128)(2,1)}, u32[]{:S(2)}) copy-start(bf16[16,1024]{1,0:T(8,128)(2,1)} %we_ref.3) | copy-start | bytes 98308
  31.8 13.7 %copy-start.7 = (s32[8,256]{1,0:T(8,128)S(1)}, s32[8,256]{1,0:T(8,128)}, u32[]{:S(2)}) copy-start(s32[8,256]{1,0:T(8,128)} %slot_ref.3) | copy-start | bytes 24580
